TPU v7x, 256 devices: a whole 4x4x8 slice. The times are simulated.
256 devices in a mesh: rows: 32 (over y, z), cols: 8 (over x, core).
Axes of the slice: x: 4, y: 4, z: 8, core: 2. Of those that a mesh axis runs over, the one named last changes fastest.
Arguments:
- genotypes: int32 [20480, 4096], P('rows', 'cols'), may hold values from 0 to 2
- frequencies: float32 [4096], P('cols'), may hold values from 0.05 to 0.5
- traits: bfloat16 [20480, 32768], P('rows', 'cols'), may hold values from -6 to 6
- geno_sketch: bfloat16 [4096, 512], P('cols'), may hold values from -0.09375 to 0.09375
- trait_sketch: bfloat16 [32768, 512], P('cols'), may hold values from -0.03125 to 0.03125
- initial: float32 [512, 256], replicated, may hold values from -6 to 6
Outputs:
- geno_scores: bfloat16 [20480, 256], P('rows')
- trait_scores: bfloat16 [20480, 256], P('rows')
- geno_loadings: float32 [256, 4096], P('rows', 'cols')
- trait_loadings: float32 [256, 32768], P('rows', 'cols')
All inputs are finite; a program needn't handle non-finite values.
Results may differ from a plain program's by a relative error of at most 0.0059.
Values sent between devices are 32-bit elements; how exact they have to be, the bound alone decides.
A program may use at most 128 MiB of HBM per device.

v0:
```python
import math
import jax
import jax.numpy as jnp
from jax import lax
from jax.sharding import PartitionSpec as P


def standard(genotypes, frequencies):
    spread = lax.rsqrt(2.0 * frequencies * (1.0 - frequencies))
    return ((genotypes.astype(jnp.float32) - 2.0 * frequencies) * spread).astype(jnp.bfloat16)


def unit_columns(matrix):
    return matrix * lax.rsqrt(jnp.mean(matrix * matrix, axis=0, keepdims=True) + 1e-06)


def inner_product(left_side, right_side):
    return lax.dot_general(
        left_side,
        right_side,
        (((0,), (0,)), ((), ())),
        precision=lax.Precision.HIGHEST,
        preferred_element_type=jnp.float32,
    )


def on_device(genotypes, frequencies, traits, geno_sketch, trait_sketch, initial):
    people = genotypes.shape[0] * lax.axis_size("rows")
    sketch_width = geno_sketch.shape[1]
    standardized = standard(genotypes, frequencies)
    partial_geno = jnp.dot(standardized, geno_sketch, preferred_element_type=jnp.float32)
    partial_trait = jnp.dot(traits, trait_sketch, preferred_element_type=jnp.float32)
    sketch_geno, sketch_trait = lax.psum((partial_geno, partial_trait), "cols")
    gram_geno, gram_trait = lax.psum(
        (inner_product(sketch_geno, sketch_geno), inner_product(sketch_trait, sketch_trait)), "rows"
    )
    lower_geno = jnp.linalg.cholesky(gram_geno / people)
    lower_trait = jnp.linalg.cholesky(gram_trait / people)
    basis_geno = lax.linalg.triangular_solve(
        lower_geno, sketch_geno, left_side=False, lower=True, transpose_a=True
    )
    basis_trait = lax.linalg.triangular_solve(
        lower_trait, sketch_trait, left_side=False, lower=True, transpose_a=True
    )
    crossed = lax.psum(inner_product(basis_geno, basis_trait), "rows") / people
    left_dirs = unit_columns(jnp.dot(crossed, initial, precision=lax.Precision.HIGHEST))
    right_dirs = unit_columns(inner_product(crossed, left_dirs))
    root_sketch = math.sqrt(sketch_width)
    geno_scores = (
        jnp.dot(basis_geno, left_dirs, precision=lax.Precision.HIGHEST) / root_sketch
    ).astype(jnp.bfloat16)
    trait_scores = (
        jnp.dot(basis_trait, right_dirs, precision=lax.Precision.HIGHEST) / root_sketch
    ).astype(jnp.bfloat16)
    geno_width = standardized.shape[1]
    geno_term = lax.dot_general(
        geno_scores, standardized, (((0,), (0,)), ((), ())), preferred_element_type=jnp.float32
    )
    trait_term = lax.dot_general(
        trait_scores, traits, (((0,), (0,)), ((), ())), preferred_element_type=jnp.float32
    )
    summed = lax.psum_scatter(
        jnp.concatenate([geno_term, trait_term], axis=1), "rows", scatter_dimension=0, tiled=True
    )
    root_people = math.sqrt(people)
    geno_loadings = summed[:, :geno_width] / root_people
    trait_loadings = summed[:, geno_width:] / root_people
    return (geno_scores, trait_scores, geno_loadings, trait_loadings)


def solution(mesh):
    placed = (
        P("rows", "cols"),
        P("cols"),
        P("rows", "cols"),
        P("cols", None),
        P("cols", None),
        P(),
    )
    return jax.shard_map(
        on_device,
        mesh=mesh,
        in_specs=placed,
        out_specs=(P("rows", None), P("rows", None), P("rows", "cols"), P("rows", "cols")),
        check_vma=False,
    )
```

profile of v0, /device:TPU:2, one launch (start us, length us, event | category | flops | bytes accessed | tf_op | source)
XLA Modules:
  0.0 961.9 jit_solution(18372460097444687967)
XLA Ops:
  8.0 7.8 fusion.85
  17.4 73.2 %all-reduce.11.cloned.1.call-done = (f32[640,512]{1,0:T(8,128)}, f32[640,512]{1,0:T(8,128)}) async-done(((f32[640,512]{1,0:T(8,128)}, f32[640,512]{1,0:T(8,128)}), (f32[640,512]{1,0:T(8,128)}, f32[640,512]{1,0:T(8,128)})) %all-reduce.11.cloned.1.call-update) | async-done | bytes 2621456 | tf_op jit(solution)/shard_map/psum | solution.py:33
  90.6 5.5 fusion.84
  100.0 156.1 %all-reduce.9.cloned.1.call-done = (f32[512,512]{0,1:T(8,128)}, f32[512,512]{0,1:T(8,128)}) async-done(((f32[512,512]{0,1:T(8,128)}, f32[512,512]{0,1:T(8,128)}), (f32[512,512]{0,1:T(8,128)}, f32[512,512]{0,1:T(8,128)})) %all-reduce.9.cloned.1.call-update) | async-done | bytes 2097168 | tf_op jit(solution)/shard_map/psum | solution.py:34
  265.1 11.7 %cholesky.358 = f32[128,128]{1,0:T(8,128)S(1)} custom-call(f32[128,128]{1,0:T(8,128)S(1)} %cholesky.439), custom_call_target="Cholesky" | custom-call | tf_op jit(solution)/shard_map/jit(cholesky)/cholesky | solution.py:38
  276.9 11.7 %cholesky.286 = f32[128,128]{1,0:T(8,128)S(1)} custom-call(f32[128,128]{1,0:T(8,128)S(1)} %cholesky.426), custom_call_target="Cholesky" | custom-call | tf_op jit(solution)/shard_map/jit(cholesky)/cholesky | solution.py:37
  289.3 10.4 %custom-call.27 = f32[1,128,128]{1,2,0:T(8,128)} custom-call(f32[1,128,128]{2,1,0:T(8,128)S(1)} %get-tuple-element.65), custom_call_target="InvertDiagBlocksLowerTriangular" | custom-call | tf_op jit(solution)/shard_map/jit(cholesky)/cholesky | solution.py:37
  300.4 10.0 %custom-call.31 = f32[1,128,128]{1,2,0:T(8,128)S(1)} custom-call(f32[1,128,128]{2,1,0:T(8,128)S(1)} %get-tuple-element.55), custom_call_target="InvertDiagBlocksLowerTriangular" | custom-call | tf_op jit(solution)/shard_map/jit(cholesky)/cholesky | solution.py:38
  313.0 11.7 %cholesky.377 = f32[128,128]{1,0:T(8,128)S(1)} custom-call(f32[128,128]{1,0:T(8,128)S(1)} %cholesky.443), custom_call_target="Cholesky" | custom-call | tf_op jit(solution)/shard_map/jit(cholesky)/cholesky | solution.py:38
  325.5 9.8 %custom-call.32 = f32[1,128,128]{1,2,0:T(8,128)S(1)} custom-call(f32[1,128,128]{2,1,0:T(8,128)S(1)} %get-tuple-element.52), custom_call_target="InvertDiagBlocksLowerTriangular" | custom-call | tf_op jit(solution)/shard_map/jit(cholesky)/cholesky | solution.py:38
  336.9 12.1 %cholesky.398 = f32[128,128]{1,0:T(8,128)S(1)} custom-call(f32[128,128]{1,0:T(8,128)S(1)} %cholesky.448), custom_call_target="Cholesky" | custom-call | tf_op jit(solution)/shard_map/jit(cholesky)/cholesky | solution.py:38
  349.7 9.8 %custom-call.33 = f32[1,128,128]{1,2,0:T(8,128)S(1)} custom-call(f32[1,128,128]{2,1,0:T(8,128)S(1)} %get-tuple-element.49), custom_call_target="InvertDiagBlocksLowerTriangular" | custom-call | tf_op jit(solution)/shard_map/jit(cholesky)/cholesky | solution.py:38
  361.0 11.7 %cholesky.415 = f32[128,128]{1,0:T(8,128)S(1)} custom-call(f32[128,128]{1,0:T(8,128)S(1)} %convolution_subtract_fusion.10), custom_call_target="Cholesky" | custom-call | tf_op jit(solution)/shard_map/jit(cholesky)/cholesky | solution.py:38
  377.0 11.7 %while.5 = (s32[]{:T(128)}, f32[512,512]{1,0:T(8,128)}, s32[4,2]{0,1:T(2,128)S(1)}, f32[4,128,128]{2,1,0:T(8,128)S(1)}, s32[]{:T(128)}) while((s32[]{:T(128)}, f32[512,512]{1,0:T(8,128)}, s32[4,2]{0,1:T(2,128)S(1)}, f32[4,128,128]{2,1,0:T(8,128)S(1)}, s32[]{:T(128)}) %tuple.61), condition=%wide.while_cond.clone, body=%wide.while_body.clone.sunk | while | flops 2 | bytes 131189 | solution.py:42
  388.7 39.5 %custom-call.34 = f32[4,128,128]{1,2,0:T(8,128)S(1)} custom-call(f32[4,128,128]{2,1,0:T(8,128)S(1)} %get-tuple-element.21), custom_call_target="InvertDiagBlocksLowerTriangular" | custom-call | tf_op jit(solution)/shard_map/triangular_solve/custom-call.3 | solution.py:42
  438.9 11.7 %cholesky.305 = f32[128,128]{1,0:T(8,128)S(1)} custom-call(f32[128,128]{1,0:T(8,128)S(1)} %cholesky.430), custom_call_target="Cholesky" | custom-call | tf_op jit(solution)/shard_map/jit(cholesky)/cholesky | solution.py:37
  451.3 9.8 %custom-call.28 = f32[1,128,128]{1,2,0:T(8,128)S(1)} custom-call(f32[1,128,128]{2,1,0:T(8,128)S(1)} %get-tuple-element.62), custom_call_target="InvertDiagBlocksLowerTriangular" | custom-call | tf_op jit(solution)/shard_map/jit(cholesky)/cholesky | solution.py:37
  462.9 11.7 %cholesky.326 = f32[128,128]{1,0:T(8,128)S(1)} custom-call(f32[128,128]{1,0:T(8,128)S(1)} %cholesky.435), custom_call_target="Cholesky" | custom-call | tf_op jit(solution)/shard_map/jit(cholesky)/cholesky | solution.py:37
  475.3 9.8 %custom-call.29 = f32[1,128,128]{1,2,0:T(8,128)S(1)} custom-call(f32[1,128,128]{2,1,0:T(8,128)S(1)} %get-tuple-element.59), custom_call_target="InvertDiagBlocksLowerTriangular" | custom-call | tf_op jit(solution)/shard_map/jit(cholesky)/cholesky | solution.py:37
  485.7 11.7 %cholesky.343 = f32[128,128]{1,0:T(8,128)S(1)} custom-call(f32[128,128]{1,0:T(8,128)S(1)} %convolution_subtract_fusion.11), custom_call_target="Cholesky" | custom-call | tf_op jit(solution)/shard_map/jit(cholesky)/cholesky | solution.py:37
  501.9 11.6 %while.4 = (s32[]{:T(128)}, f32[512,512]{1,0:T(8,128)}, s32[4,2]{0,1:T(2,128)S(1)}, f32[4,128,128]{2,1,0:T(8,128)S(1)}, s32[]{:T(128)}) while((s32[]{:T(128)}, f32[512,512]{1,0:T(8,128)}, s32[4,2]{0,1:T(2,128)S(1)}, f32[4,128,128]{2,1,0:T(8,128)S(1)}, s32[]{:T(128)}) %tuple.74), condition=%wide.while_cond, body=%wide.while_body.sunk | while | flops 2 | bytes 131189 | solution.py:39
  513.5 39.7 %custom-call.30 = f32[4,128,128]{1,2,0:T(8,128)S(1)} custom-call(f32[4,128,128]{2,1,0:T(8,128)S(1)} %get-tuple-element.20), custom_call_target="InvertDiagBlocksLowerTriangular" | custom-call | tf_op jit(solution)/shard_map/triangular_solve/custom-call.3 | solution.py:39
  567.6 147.0 %all-reduce.7.cloned.1.call-done = f32[512,512]{0,1:T(8,128)} async-done(((f32[512,512]{0,1:T(8,128)}), f32[512,512]{0,1:T(8,128)}) %all-reduce.7.cloned.1.call-update) | async-done | bytes 1048592 | tf_op jit(solution)/shard_map/psum | solution.py:45
  730.9 221.3 %reduce-scatter.2.cloned.1.call-done = f32[8,4608]{1,0:T(8,128)} async-done(((f32[256,4608]{1,0:T(8,128)}), f32[8,4608]{1,0:T(8,128)}) %reduce-scatter.2.cloned.1.call-update) | async-done | bytes 147472 | tf_op jit(solution)/shard_map/reduce_scatter | solution.py:62
  (159 shorter events, 98.1 us)
Async XLA Ops:
  7.2 8.6 copy-start
  7.2 83.4 %all-reduce.11.cloned.1.call-start = ((), (), s32[]{:S(2)}) async-start(), calls=%async_computation.4 | async-start | bytes 5242880 | tf_op jit(solution)/shard_map/psum | solution.py:33
  8.0 7.8 copy-start.3
  17.4 238.7 %all-reduce.9.cloned.1.call-start = ((), (), s32[]{:S(2)}) async-start(), calls=%async_computation.3 | async-start | bytes 4194304 | tf_op jit(solution)/shard_map/psum | solution.py:34
  90.6 5.5 copy-start.2
  99.8 614.8 %all-reduce.7.cloned.1.call-start = ((), (), s32[]{:S(2)}) async-start(), calls=%async_computation.1 | async-start | bytes 2097152 | tf_op jit(solution)/shard_map/psum | solution.py:45
  264.2 36.2 %copy-start.6 = (f32[512,512]{1,0:T(8,128)}, f32[512,512]{1,0:T(8,128)S(1)}, u32[]{:S(2)}) copy-start(f32[512,512]{1,0:T(8,128)S(1)} %get-tuple-element.77) | copy-start | bytes 3145732
  288.6 23.2 %copy-start.18 = (f32[128,128]{1,0:T(8,128)}, f32[128,128]{1,0:T(8,128)S(1)}, u32[]{:S(2)}) copy-start(f32[128,128]{1,0:T(8,128)S(1)} %cholesky.286) | copy-start | bytes 196612
  433.3 2.8 copy-start.9
  433.3 4.1 copy-start.19
  436.2 1.4 copy-start.7
  436.2 1.4 copy-start.22
  500.8 52.5 %copy-start.1 = (f32[640,512]{1,0:T(8,128)S(1)}, f32[640,512]{1,0:T(8,128)}, u32[]{:S(2)}) copy-start(f32[640,512]{1,0:T(8,128)} %get-tuple-element.40) | copy-start | bytes 3932164
  555.5 3.5 copy-start.21
  559.5 3.4 copy-start.11
  559.5 4.1 copy-start.10
  559.5 4.1 copy-start.14
  563.6 162.8 %slice-start = ((s8[5242880]{0:T(1024)(128)(4,1)}), s8[1048576]{0:T(1024)(128)(4,1)S(1)}, s32[]{:S(2)}) async-start(s8[5242880]{0:T(1024)(128)(4,1)} %bitcast.109), calls=%async_computation.5 | async-start | bytes 2097152
  567.3 384.9 %reduce-scatter.2.cloned.1.call-start = ((), (), s32[]{:S(2)}) async-start(), calls=%async_computation.2 | async-start | bytes 4866048 | tf_op jit(solution)/shard_map/reduce_scatter | solution.py:62
  714.6 6.8 copy-start.5
  714.6 7.9 copy-start.4
  718.0 8.5 slice-start.1
  721.5 1.5 copy-start.17
  722.5 1.0 copy-start.15
  (5 other events, 3.8 us)
Sparse Core Ops, SparseCore 0:
  17.5 73.0 all-reduce.10
  99.9 156.1 all-reduce.8
  567.5 147.0 all-reduce.6
  731.0 221.1 reduce-scatter.1
where the time goes:
time: 969 us; the launch traced here: 962 us
  waiting for transfers between devices  598 us (62%)
  other arithmetic  252 us (26%)
  matrix products  61.5 us (6%)
  local copies, waits for them, and re-layouts  29.9 us (3%)
  between operations  19.7 us (2%)
    reduce_scatter x1, waiting for transfers between devices, on_device(): lax.psum_scatter(jnp.concatenate([geno_term, trait_term], axis=1), 'rows'...  221 us
    psum x1, waiting for transfers between devices, on_device(): lax.psum((inner_product(sketch_geno, sketch_geno), inner_product(sketch_t...  156 us
    psum x1, waiting for transfers between devices, on_device(): crossed = lax.psum(inner_product(basis_geno, basis_trait), 'rows') / people  147 us
    another operation x15, other arithmetic, on_device(): lower_trait = jnp.linalg.cholesky(gram_trait / people)  79.7 us
    another operation x15, other arithmetic, on_device(): lower_geno = jnp.linalg.cholesky(gram_geno / people)  79.7 us
    psum x1, waiting for transfers between devices, on_device(): sketch_geno, sketch_trait = lax.psum((partial_geno, partial_trait), 'cols')  73.2 us
    another operation x3, other arithmetic, on_device(): lax.linalg.triangular_solve(lower_geno, sketch_geno, left_side=False, low...  40.8 us
    another operation x2, other arithmetic, on_device(): lax.linalg.triangular_solve(lower_trait, sketch_trait, left_side=False, l...  40.6 us
  transfers between devices with their start and end apart: 4, of which 4 were waited for; matrix products, arithmetic and copies ran while one was open for 0% of the time, Pallas kernels for 0%

commit v1 on v0

--- a/solution.py
+++ b/solution.py
@@ -42,7 +42,9 @@
     basis_trait = lax.linalg.triangular_solve(
         lower_trait, sketch_trait, left_side=False, lower=True, transpose_a=True
     )
-    crossed = lax.psum(inner_product(basis_geno, basis_trait), "rows") / people
+    crossed = (
+        jnp.sum(lax.all_gather(inner_product(basis_geno, basis_trait), "rows"), axis=0) / people
+    )
     left_dirs = unit_columns(jnp.dot(crossed, initial, precision=lax.Precision.HIGHEST))
     right_dirs = unit_columns(inner_product(crossed, left_dirs))
     root_sketch = math.sqrt(sketch_width)

time: 969 us -> 1060 us (1.094)
  waiting for transfers between devices: 598 us -> 681 us
  other arithmetic: 252 us -> 266 us
    all_gather x0 -> x1, waiting for transfers between devices: none -> 231 us  [on_device(): lax.all_gather(inner_product(basis_geno, basis_trait), 'rows')]
    psum x1 -> x0, waiting for transfers between devices: 147 us -> none  [on_device(): crossed = lax.psum(inner_product(basis_geno, basis_trait), 'rows') / people]
    reduce_sum x0 -> x1, other arithmetic: none -> 13.5 us  [on_device(): jnp.sum(lax.all_gather(inner_product(basis_geno, basis_trait), 'rows'), a...]
where the time goes in v1:
time: 1060 us
  waiting for transfers between devices  681 us (64%)
  other arithmetic  266 us (25%)
  matrix products  58 us (5%)
  local copies, waits for them, and re-layouts  30.2 us (3%)
  between operations  19.7 us (2%)
    all_gather x1, waiting for transfers between devices, on_device(): lax.all_gather(inner_product(basis_geno, basis_trait), 'rows')  231 us
    reduce_scatter x1, waiting for transfers between devices, on_device(): lax.psum_scatter(jnp.concatenate([geno_term, trait_term], axis=1), 'rows'...  221 us
    psum x1, waiting for transfers between devices, on_device(): lax.psum((inner_product(sketch_geno, sketch_geno), inner_product(sketch_t...  156 us
    another operation x15, other arithmetic, on_device(): lower_geno = jnp.linalg.cholesky(gram_geno / people)  79.6 us
    another operation x15, other arithmetic, on_device(): lower_trait = jnp.linalg.cholesky(gram_trait / people)  79.5 us
    psum x1, waiting for transfers between devices, on_device(): sketch_geno, sketch_trait = lax.psum((partial_geno, partial_trait), 'cols')  73.2 us
    another operation x3, other arithmetic, on_device(): lax.linalg.triangular_solve(lower_geno, sketch_geno, left_side=False, low...  40.6 us
    another operation x2, other arithmetic, on_device(): lax.linalg.triangular_solve(lower_trait, sketch_trait, left_side=False, l...  40.4 us
  transfers between devices with their start and end apart: 4, of which 4 were waited for; matrix products, arithmetic and copies ran while one was open for 0% of the time, Pallas kernels for 0%

profile of v1, /device:TPU:2, one launch (start us, length us, event | category | flops | bytes accessed | tf_op | source)
XLA Modules:
  0.0 1055.7 jit_solution(6625407718366776130)
XLA Ops:
  8.0 7.8 fusion.85
  17.4 73.2 %all-reduce.8.cloned.1.call-done = (f32[640,512]{1,0:T(8,128)}, f32[640,512]{1,0:T(8,128)}) async-done(((f32[640,512]{1,0:T(8,128)}, f32[640,512]{1,0:T(8,128)}), (f32[640,512]{1,0:T(8,128)}, f32[640,512]{1,0:T(8,128)})) %all-reduce.8.cloned.1.call-update) | async-done | bytes 2621456 | tf_op jit(solution)/shard_map/psum | solution.py:33
  100.1 156.0 %all-reduce.6.cloned.1.call-done = (f32[512,512]{0,1:T(8,128)}, f32[512,512]{0,1:T(8,128)}) async-done(((f32[512,512]{0,1:T(8,128)}, f32[512,512]{0,1:T(8,128)}), (f32[512,512]{0,1:T(8,128)}, f32[512,512]{0,1:T(8,128)})) %all-reduce.6.cloned.1.call-update) | async-done | bytes 2097168 | tf_op jit(solution)/shard_map/psum | solution.py:34
  266.0 11.7 %cholesky.358 = f32[128,128]{1,0:T(8,128)S(1)} custom-call(f32[128,128]{1,0:T(8,128)S(1)} %cholesky.439), custom_call_target="Cholesky" | custom-call | tf_op jit(solution)/shard_map/jit(cholesky)/cholesky | solution.py:38
  277.8 9.8 custom-call.31
  290.2 11.7 %cholesky.377 = f32[128,128]{1,0:T(8,128)S(1)} custom-call(f32[128,128]{1,0:T(8,128)S(1)} %cholesky.443), custom_call_target="Cholesky" | custom-call | tf_op jit(solution)/shard_map/jit(cholesky)/cholesky | solution.py:38
  303.2 10.2 custom-call.32
  315.0 11.7 %cholesky.398 = f32[128,128]{1,0:T(8,128)S(1)} custom-call(f32[128,128]{1,0:T(8,128)S(1)} %cholesky.448), custom_call_target="Cholesky" | custom-call | tf_op jit(solution)/shard_map/jit(cholesky)/cholesky | solution.py:38
  327.4 9.8 custom-call.33
  338.6 11.9 %cholesky.415 = f32[128,128]{1,0:T(8,128)S(1)} custom-call(f32[128,128]{1,0:T(8,128)S(1)} %convolution_subtract_fusion.10), custom_call_target="Cholesky" | custom-call | tf_op jit(solution)/shard_map/jit(cholesky)/cholesky | solution.py:38
  354.8 11.6 %while.5 = (s32[]{:T(128)}, f32[512,512]{1,0:T(8,128)}, s32[4,2]{0,1:T(2,128)S(1)}, f32[4,128,128]{2,1,0:T(8,128)S(1)}, s32[]{:T(128)}) while((s32[]{:T(128)}, f32[512,512]{1,0:T(8,128)}, s32[4,2]{0,1:T(2,128)S(1)}, f32[4,128,128]{2,1,0:T(8,128)S(1)}, s32[]{:T(128)}) %tuple.61), condition=%wide.while_cond.clone, body=%wide.while_body.clone.sunk | while | flops 2 | bytes 131181 | solution.py:42
  366.4 39.3 %custom-call.34 = f32[4,128,128]{1,2,0:T(8,128)S(1)} custom-call(f32[4,128,128]{2,1,0:T(8,128)S(1)} %get-tuple-element.21), custom_call_target="InvertDiagBlocksLowerTriangular" | custom-call | tf_op jit(solution)/shard_map/triangular_solve/custom-call.3 | solution.py:42
  415.8 11.7 %cholesky.286 = f32[128,128]{1,0:T(8,128)S(1)} custom-call(f32[128,128]{1,0:T(8,128)S(1)} %cholesky.426), custom_call_target="Cholesky" | custom-call | tf_op jit(solution)/shard_map/jit(cholesky)/cholesky | solution.py:37
  427.5 9.8 custom-call.27
  438.1 11.9 %cholesky.305 = f32[128,128]{1,0:T(8,128)S(1)} custom-call(f32[128,128]{1,0:T(8,128)S(1)} %cholesky.430), custom_call_target="Cholesky" | custom-call | tf_op jit(solution)/shard_map/jit(cholesky)/cholesky | solution.py:37
  451.4 9.8 custom-call.28
  461.8 11.7 %cholesky.326 = f32[128,128]{1,0:T(8,128)S(1)} custom-call(f32[128,128]{1,0:T(8,128)S(1)} %cholesky.435), custom_call_target="Cholesky" | custom-call | tf_op jit(solution)/shard_map/jit(cholesky)/cholesky | solution.py:37
  474.2 10.2 custom-call.29
  485.0 11.7 %cholesky.343 = f32[128,128]{1,0:T(8,128)S(1)} custom-call(f32[128,128]{1,0:T(8,128)S(1)} %convolution_subtract_fusion.11), custom_call_target="Cholesky" | custom-call | tf_op jit(solution)/shard_map/jit(cholesky)/cholesky | solution.py:37
  501.2 11.6 %while.4 = (s32[]{:T(128)}, f32[512,512]{1,0:T(8,128)}, s32[4,2]{0,1:T(2,128)S(1)}, f32[4,128,128]{2,1,0:T(8,128)S(1)}, s32[]{:T(128)}) while((s32[]{:T(128)}, f32[512,512]{1,0:T(8,128)}, s32[4,2]{0,1:T(2,128)S(1)}, f32[4,128,128]{2,1,0:T(8,128)S(1)}, s32[]{:T(128)}) %tuple.74), condition=%wide.while_cond, body=%wide.while_body.sunk | while | flops 2 | bytes 131181 | solution.py:39
  512.7 39.5 %custom-call.30 = f32[4,128,128]{1,2,0:T(8,128)S(1)} custom-call(f32[4,128,128]{2,1,0:T(8,128)S(1)} %get-tuple-element.20), custom_call_target="InvertDiagBlocksLowerTriangular" | custom-call | tf_op jit(solution)/shard_map/triangular_solve/custom-call.3 | solution.py:39
  565.4 231.0 %all-gather.3.cloned.1.call-done = f32[16384,512]{1,0:T(8,128)} async-done(((f32[512,512]{1,0:T(8,128)}), f32[16384,512]{1,0:T(8,128)}) %all-gather.3.cloned.1.call-update) | async-done | bytes 33554448 | tf_op jit(solution)/shard_map/all_gather | solution.py:46
  796.3 13.5 %reduce_sum.27 = f32[512,512]{1,0:T(8,128)} reduce(f32[32,512,512]{2,1,0:T(8,128)} %bitcast.110, f32[]{:T(128)} %constant.122.clone.1), dimensions={0}, to_apply=%region_12.15 | reduce | flops 8126464 | bytes 34603012 | tf_op jit(solution)/shard_map/reduce_sum | solution.py:46
  825.1 221.0 %reduce-scatter.2.cloned.1.call-done = f32[8,4608]{1,0:T(8,128)} async-done(((f32[256,4608]{1,0:T(8,128)}), f32[8,4608]{1,0:T(8,128)}) %reduce-scatter.2.cloned.1.call-update) | async-done | bytes 147472 | tf_op jit(solution)/shard_map/reduce_scatter | solution.py:64
  (157 shorter events, 101.1 us)
Async XLA Ops:
  7.2 8.6 copy-start
  7.2 83.5 %all-reduce.8.cloned.1.call-start = ((), (), s32[]{:S(2)}) async-start(), calls=%async_computation.4 | async-start | bytes 5242880 | tf_op jit(solution)/shard_map/psum | solution.py:33
  8.0 7.8 copy-start.4
  17.4 238.6 %all-reduce.6.cloned.1.call-start = ((), (), s32[]{:S(2)}) async-start(), calls=%async_computation.3 | async-start | bytes 4194304 | tf_op jit(solution)/shard_map/psum | solution.py:34
  90.6 5.5 copy-start.3
  99.8 696.5 %all-gather.3.cloned.1.call-start = ((), (), s32[]{:S(2)}) async-start(), calls=%async_computation.2 | async-start | bytes 34603008 | tf_op jit(solution)/shard_map/all_gather | solution.py:46
  410.9 4.9 copy-start.10
  413.7 23.8 %copy-start.8 = (f32[512,512]{1,0:T(8,128)S(1)}, f32[512,512]{1,0:T(8,128)}, u32[]{:S(2)}) copy-start(f32[512,512]{1,0:T(8,128)} %get-tuple-element.77) | copy-start | bytes 3145732
  500.0 52.2 %copy-start.2 = (f32[640,512]{1,0:T(8,128)S(1)}, f32[640,512]{1,0:T(8,128)}, u32[]{:S(2)}) copy-start(f32[640,512]{1,0:T(8,128)} %get-tuple-element.40) | copy-start | bytes 3932164
  554.8 6.1 copy-start.6
  557.5 3.4 copy-start.13
  557.5 4.1 copy-start.11
  557.5 4.1 copy-start.16
  565.3 480.7 %reduce-scatter.2.cloned.1.call-start = ((), (), s32[]{:S(2)}) async-start(), calls=%async_computation.1 | async-start | bytes 4866048 | tf_op jit(solution)/shard_map/reduce_scatter | solution.py:64
  809.8 10.3 slice-start
  811.4 4.1 copy-start.14
  811.4 4.1 copy-start.19
  811.4 6.4 copy-start.17
  814.4 5.6 slice-start.1
  815.5 2.3 copy-start.12
  817.8 4.2 copy-start.20
  820.1 1.9 copy-start.15
  820.1 1.9 copy-start.5
  825.0 223.9 %copy-start.1 = (bf16[512,512]{1,0:T(8,128)(2,1)S(1)}, bf16[512,512]{1,0:T(8,128)(2,1)}, u32[]{:S(2)}) copy-start(bf16[512,512]{1,0:T(8,128)(2,1)} %param.12) | copy-start | bytes 1572868
  (3 other events, 2.8 us)
Sparse Core Ops, SparseCore 0:
  17.5 73.0 all-reduce.7
  100.0 156.0 all-reduce.5
  565.4 230.8 all-gather.2
  825.2 220.8 reduce-scatter.1
